TPU v7x, 128 devices: a whole 4x4x4 slice. The times are simulated.
128 devices in a mesh: seq: 32 (over y, z, core), head: 4 (over x).
Axes of the slice: x: 4, y: 4, z: 4, core: 2. Of those that a mesh axis runs over, the one named last changes fastest.
Arguments:
- vision: bfloat16 [65536, 7680], P(('seq', 'head')), may hold values from -6 to 6
- w_key: bfloat16 [7680, 512], replicated, may hold values from -0.0625 to 0.0625
- w_value: bfloat16 [7680, 512], replicated, may hold values from -0.0625 to 0.0625
- queries: bfloat16 [256, 4096], P('seq', 'head'), may hold values from -240 to 240
- w_out: bfloat16 [4096, 8192], P('head', 'seq'), may hold values from -0.09375 to 0.09375
Outputs:
- mixed: bfloat16 [256, 8192], P('head', 'seq')
All inputs are finite; a program needn't handle non-finite values.
Results may differ from a plain program's by a relative error of at most 0.03.
Values may be sent and summed in bfloat16 or wider, within the bound.
No kernel may reach another device: no remote copies, remote signals or barrier semaphores. Data moves between devices by JAX's collectives and lax.ppermute only.
A program may use at most 128 MiB of HBM per device.

v0:
```python
import jax
import jax.numpy as jnp
from jax import lax
from jax.sharding import PartitionSpec as P

HD = 128


def scale_rows(partial_value, factor):
    return (
        partial_value.reshape(factor.shape[0], factor.shape[1], -1) * factor[:, :, None]
    ).reshape(factor.shape[0], -1)


def divide_rows(partial_value, denom):
    return (partial_value.reshape(denom.shape[0], denom.shape[1], -1) / denom[:, :, None]).reshape(
        denom.shape[0], -1
    )


def attend(queries_all, keys_here, values_here):
    head_size = HD
    kv_local = keys_here.shape[1] // head_size
    text_rows = queries_all.shape[0]
    q_heads = queries_all.shape[1] // head_size
    group_size = q_heads // kv_local
    grouped = queries_all.reshape(text_rows, kv_local, group_size, head_size)
    key_heads = keys_here.reshape(keys_here.shape[0], kv_local, head_size)
    value_heads = values_here.reshape(values_here.shape[0], kv_local, head_size)
    scores = jnp.einsum(
        "tkgd,nkd->kgtn", grouped, key_heads, preferred_element_type=jnp.float32
    ) * head_size ** (-0.5)
    maxima = jnp.max(scores, axis=-1)
    powers = jnp.exp(scores - maxima[..., None])
    totals = jnp.sum(powers, axis=-1)
    partial_value = jnp.einsum(
        "kgtn,nkd->tkgd",
        powers.astype(jnp.bfloat16),
        value_heads,
        preferred_element_type=jnp.float32,
    )
    partial_value = partial_value.reshape(text_rows, q_heads * head_size)
    maxima = maxima.transpose(2, 0, 1).reshape(text_rows, q_heads)
    totals = totals.transpose(2, 0, 1).reshape(text_rows, q_heads)
    return (maxima, totals, partial_value)


def shards(vision, w_key, w_value, queries, w_out):
    keys = jnp.dot(vision, w_key, preferred_element_type=jnp.float32).astype(jnp.bfloat16)
    values = jnp.dot(vision, w_value, preferred_element_type=jnp.float32).astype(jnp.bfloat16)
    keys_here, values_here = (
        lax.all_to_all(keys, "head", split_axis=1, concat_axis=0, tiled=True),
        lax.all_to_all(values, "head", split_axis=1, concat_axis=0, tiled=True),
    )
    queries_all = lax.all_gather(queries, "seq", axis=0, tiled=True)
    maxima, totals, partial_value = attend(queries_all, keys_here, values_here)
    global_max = lax.pmax(maxima, "seq")
    factor = jnp.exp(maxima - global_max)
    denom, numer = (
        lax.psum((totals * factor).astype(jnp.bfloat16), "seq").astype(jnp.float32),
        lax.psum(scale_rows(partial_value, factor).astype(jnp.bfloat16), "seq").astype(jnp.float32),
    )
    attended = divide_rows(numer, denom).astype(jnp.bfloat16)
    return lax.psum_scatter(
        jnp.dot(attended, w_out, preferred_element_type=jnp.float32).astype(jnp.bfloat16),
        "head",
        scatter_dimension=0,
        tiled=True,
    )


def solution(mesh):
    placed = (P(("seq", "head"), None), P(), P(), P("seq", "head"), P("head", "seq"))
    return jax.shard_map(
        shards, mesh=mesh, in_specs=placed, out_specs=P("head", "seq"), check_vma=False
    )
```

profile of v0, /device:TPU:0, one launch (start us, length us, event | category | flops | bytes accessed | tf_op | source)
XLA Modules:
  0.0 286.8 jit_solution(6718358822578115209)
XLA Ops:
  6.5 0.0 copy-start
  6.5 10.6 %convolution_convert_fusion.1 = bf16[512,512]{0,1:T(8,128)(2,1)} fusion(bf16[512,7680]{1,0:T(8,128)(2,1)} %param.5, bf16[7680,512]{1,0:T(8,128)(2,1)} %param.7), kind=kOutput, calls=%fused_computation.8 | convolution fusion | flops 4026793984 | bytes 16252928 | tf_op jit(solution)/shard_map/dot_general | solution.py:50
  17.1 0.0 copy-start.1
  17.1 4.5 %all-to-all-start = ((bf16[512,4,128]{0,2,1:T(8,128)(2,1)}), bf16[512,4,128]{0,2,1:T(8,128)(2,1)S(1)}, u32[]{:S(2)}, u32[]{:S(2)}) async-start(bf16[512,4,128]{0,2,1:T(8,128)(2,1)} %bitcast), calls=%async_computation | async-start | bytes 1048576 | tf_op jit(solution)/shard_map/all_to_all | solution.py:53
  21.7 10.5 %convolution_convert_fusion = bf16[512,512]{0,1:T(8,128)(2,1)} fusion(bf16[512,7680]{1,0:T(8,128)(2,1)} %param.5, bf16[7680,512]{1,0:T(8,128)(2,1)} %param.6), kind=kOutput, calls=%fused_computation.7 | convolution fusion | flops 4026793984 | bytes 16252928 | tf_op jit(solution)/shard_map/dot_general | solution.py:49
  32.2 0.0 all-to-all-done
  32.2 4.8 %all-to-all-start.1 = ((bf16[512,4,128]{0,2,1:T(8,128)(2,1)}), bf16[512,4,128]{0,2,1:T(8,128)(2,1)S(1)}, u32[]{:S(2)}, u32[]{:S(2)}) async-start(bf16[512,4,128]{0,2,1:T(8,128)(2,1)} %bitcast.2), calls=%async_computation.1 | async-start | bytes 1048576 | tf_op jit(solution)/shard_map/all_to_all | solution.py:52
  37.0 0.0 all-reduce.2.cloned.1.call-start
  37.0 0.0 copy-done.1
  37.0 26.5 %all_gather.3 = bf16[256,1024]{1,0:T(8,128)(2,1)S(1)} all-gather(bf16[8,1024]{1,0:T(8,128)(2,1)S(1)} %copy-done.1), channel_id=1, replica_groups=mesh['seq'=32,'head'=4] {'seq'}, dimensions={0}, use_global_device_ids=true | all-gather | bytes 540672 | tf_op jit(solution)/shard_map/all_gather | solution.py:55
  63.5 0.2 copy.16
  63.7 0.4 copy.14
  64.1 0.4 reshape.57
  64.5 0.0 all-to-all-done.1
  64.5 0.3 copy.15
  64.8 8.0 %bitcast_reduce_fusion = (f32[8,256]{1,0:T(8,128)S(1)}, f32[2048,256,8]{1,0,2:T(8,128)}) fusion(bf16[2048,128,1]{1,0,2:T(8,128)(2,1)S(1)} %bitcast.66, bf16[256,8,128]{0,2,1:T(8,128)(2,1)S(1)} %bitcast.65), kind=kOutput, calls=%fused_computation.1 | convolution fusion | flops 1082128384 | bytes 17833984 | tf_op jit(solution)/shard_map/tkgd,nkd->kgtn/dot_general | solution.py:30
  72.8 8.5 %fusion.1 = f32[8,256]{1,0:T(8,128)S(1)} fusion(f32[2048,256,8]{1,0,2:T(8,128)} %get-tuple-element.8, f32[8,256]{1,0:T(8,128)S(1)} %get-tuple-element.7), kind=kLoop, calls=%fused_computation.3 | loop fusion | flops 12580864 | bytes 16793600 | tf_op jit(solution)/shard_map/reduce_sum | solution.py:35
  81.3 7.4 %fusion.4 = f32[128,8,256]{2,0,1:T(8,128)S(1)} fusion(bf16[2048,128,1]{0,1,2:T(8,128)(2,1)S(1)} %reshape.57, f32[2048,256,8]{1,0,2:T(8,128)} %get-tuple-element.8, f32[8,256]{1,0:T(8,128)S(1)} %get-tuple-element.7), kind=kOutput, calls=%fused_computation.6 | convolution fusion | flops 1086324736 | bytes 18358272 | tf_op jit(solution)/shard_map/kgtn,nkd->tkgd/dot_general | solution.py:36
  88.7 66.3 %pmax.7 = f32[256,8]{0,1:T(8,128)S(1)} all-reduce(f32[256,8]{0,1:T(8,128)S(1)} %bitcast.69), channel_id=1, replica_groups=mesh['seq'=32,'head'=4] {'seq'}, use_global_device_ids=true, to_apply=%region_1.0 | all-reduce | flops 2048 | bytes 16384 | tf_op jit(solution)/shard_map/pmax | solution.py:57
  155.1 0.9 fusion.6
  156.0 0.0 all-reduce.2.cloned.1.call-update
  156.0 0.0 reduce-scatter.2.cloned.1.call-start
  156.0 62.8 %psum.15 = bf16[256,8]{0,1:T(8,128)(2,1)S(1)} all-reduce(bf16[256,8]{0,1:T(8,128)(2,1)S(1)} %get-tuple-element.5), channel_id=1, replica_groups=mesh['seq'=32,'head'=4] {'seq'}, use_global_device_ids=true, to_apply=%region_4.0 | all-reduce | flops 2048 | bytes 8192 | tf_op jit(solution)/shard_map/psum | solution.py:60
  218.8 38.6 %all-reduce.2.cloned.1.call-done = bf16[256,1024]{0,1:T(8,128)(2,1)} async-done(((bf16[256,1024]{0,1:T(8,128)(2,1)}), bf16[256,1024]{0,1:T(8,128)(2,1)}) %all-reduce.2.cloned.1.call-update) | async-done | bytes 524304 | tf_op jit(solution)/shard_map/psum | solution.py:61
  257.4 1.1 fusion.7
  258.6 0.0 copy-done
  258.6 1.0 convolution_convert_fusion.2
  259.6 0.0 reduce-scatter.2.cloned.1.call-update
  259.6 20.4 %reduce-scatter.2.cloned.1.call-done = bf16[64,256]{1,0:T(8,128)(2,1)} async-done(((bf16[256,256]{1,0:T(8,128)(2,1)}), bf16[64,256]{1,0:T(8,128)(2,1)}) %reduce-scatter.2.cloned.1.call-update) | async-done | bytes 32784 | tf_op jit(solution)/shard_map/reduce_scatter | solution.py:64
  (2 shorter events, 0.0 us)
Async XLA Ops:
  6.5 252.0 %copy-start = (bf16[1024,256]{1,0:T(8,128)(2,1)S(1)}, bf16[1024,256]{1,0:T(8,128)(2,1)}, u32[]{:S(2)}) copy-start(bf16[1024,256]{1,0:T(8,128)(2,1)} %param.9) | copy-start | bytes 1572868
  17.1 19.9 %copy-start.1 = (bf16[8,1024]{1,0:T(8,128)(2,1)S(1)}, bf16[8,1024]{1,0:T(8,128)(2,1)}, u32[]{:S(2)}) copy-start(bf16[8,1024]{1,0:T(8,128)(2,1)} %param.8) | copy-start | bytes 49156
  17.1 15.1 %all-to-all-start = ((bf16[512,4,128]{0,2,1:T(8,128)(2,1)}), bf16[512,4,128]{0,2,1:T(8,128)(2,1)S(1)}, u32[]{:S(2)}, u32[]{:S(2)}) async-start(bf16[512,4,128]{0,2,1:T(8,128)(2,1)} %bitcast), calls=%async_computation | async-start | bytes 1048576 | tf_op jit(solution)/shard_map/all_to_all | solution.py:53
  32.2 32.3 %all-to-all-start.1 = ((bf16[512,4,128]{0,2,1:T(8,128)(2,1)}), bf16[512,4,128]{0,2,1:T(8,128)(2,1)S(1)}, u32[]{:S(2)}, u32[]{:S(2)}) async-start(bf16[512,4,128]{0,2,1:T(8,128)(2,1)} %bitcast.2), calls=%async_computation.1 | async-start | bytes 1048576 | tf_op jit(solution)/shard_map/all_to_all | solution.py:52
  37.0 220.4 %all-reduce.2.cloned.1.call-start = ((), (), s32[]{:S(2)}) async-start(), calls=%async_computation.3 | async-start | bytes 1048576 | tf_op jit(solution)/shard_map/psum | solution.py:61
  156.0 124.0 %reduce-scatter.2.cloned.1.call-start = ((), (), s32[]{:S(2)}) async-start(), calls=%async_computation.4 | async-start | bytes 163840 | tf_op jit(solution)/shard_map/reduce_scatter | solution.py:64
Sparse Core Ops, SparseCore 0:
  156.1 101.2 all-reduce.1
  259.8 20.1 reduce-scatter.1
where the time goes:
time: 287 us
  blocking collectives  156 us (54%)
  waiting for transfers between devices  59 us (21%)
  matrix products  37.6 us (13%)
  between operations  13.5 us (5%)
  other arithmetic  10.5 us (4%)
  starting transfers between devices  9.38 us (3%)
    pmax x1, blocking collectives, shards(): global_max = lax.pmax(maxima, 'seq')  66.3 us
    psum x1, blocking collectives, shards(): lax.psum((totals * factor).astype(jnp.bfloat16), 'seq').astype(jnp.float32)  62.8 us
    psum x1, waiting for transfers between devices, shards(): lax.psum(scale_rows(partial_value, factor).astype(jnp.bfloat16), 'seq')  38.6 us
    all_gather x1, blocking collectives, shards(): queries_all = lax.all_gather(queries, 'seq', axis=0, tiled=True)  26.5 us
    reduce_scatter x1, waiting for transfers between devices, shards(): lax.psum_scatter(jnp.dot(attended, w_out, preferred_element_type=jnp.floa...  20.4 us
    dot_general x1, matrix products, shards(): jnp.dot(vision, w_value, preferred_element_type=jnp.float32)  10.6 us
    dot_general x1, matrix products, shards(): jnp.dot(vision, w_key, preferred_element_type=jnp.float32)  10.5 us
    reduce_sum x1, other arithmetic, attend(): totals = jnp.sum(powers, axis=-1)  8.48 us
  transfers between devices with their start and end apart: 4, of which 2 were waited for; matrix products, arithmetic and copies ran while one was open for 4% of the time, Pallas kernels for 0%

commit v1 on v0

--- a/solution.py
+++ b/solution.py
@@ -1,9 +1,19 @@
+import functools
 import jax
 import jax.numpy as jnp
 from jax import lax
 from jax.sharding import PartitionSpec as P
+from jax.lax import all_gather
 
 HD = 128
+
+
+def prepare_rounds(here_x, named_axis):
+    current_value = jnp.sum(all_gather(here_x, named_axis), 0)
+    return current_value
+
+
+_search_racks = functools.partial(prepare_rounds, named_axis="seq")
 
 
 def scale_rows(partial_value, factor):
@@ -58,7 +68,7 @@
     factor = jnp.exp(maxima - global_max)
     denom, numer = (
         lax.psum((totals * factor).astype(jnp.bfloat16), "seq").astype(jnp.float32),
-        lax.psum(scale_rows(partial_value, factor).astype(jnp.bfloat16), "seq").astype(jnp.float32),
+        _search_racks(scale_rows(partial_value, factor).astype(jnp.bfloat16)).astype(jnp.float32),
     )
     attended = divide_rows(numer, denom).astype(jnp.bfloat16)
     return lax.psum_scatter(

time: 287 us -> 267 us (0.930)
  waiting for transfers between devices: 59 us -> 25.1 us
  other arithmetic: 10.5 us -> 18.6 us
  local copies, waits for them, and re-layouts: 1.27 us -> 4.65 us
    psum x1 -> x0, waiting for transfers between devices: 38.6 us -> none  [shards(): lax.psum(scale_rows(partial_value, factor).astype(jnp.bfloat16), 'seq')]
    reduce_sum x0 -> x1, other arithmetic: none -> 9.07 us  [prepare_rounds(): current_value = jnp.sum(all_gather(here_x, named_axis), 0)]
    all_gather x0 -> x1, waiting for transfers between devices: none -> 5.12 us  [prepare_rounds(): current_value = jnp.sum(all_gather(here_x, named_axis), 0)]
where the time goes in v1:
time: 267 us; the launch traced here: 266 us
  blocking collectives  158 us (59%)
  matrix products  37.5 us (14%)
  waiting for transfers between devices  25.1 us (9%)
  other arithmetic  18.6 us (7%)
  between operations  13.5 us (5%)
  starting transfers between devices  9.38 us (4%)
  local copies, waits for them, and re-layouts  4.65 us (2%)
    pmax x1, blocking collectives, shards(): global_max = lax.pmax(maxima, 'seq')  66.3 us
    psum x1, blocking collectives, shards(): lax.psum((totals * factor).astype(jnp.bfloat16), 'seq').astype(jnp.float32)  64.8 us
    all_gather x1, blocking collectives, shards(): queries_all = lax.all_gather(queries, 'seq', axis=0, tiled=True)  26.5 us
    reduce_scatter x1, waiting for transfers between devices, shards(): lax.psum_scatter(jnp.dot(attended, w_out, preferred_element_type=jnp.floa...  19.9 us
    dot_general x1, matrix products, shards(): jnp.dot(vision, w_key, preferred_element_type=jnp.float32)  10.6 us
    dot_general x1, matrix products, shards(): jnp.dot(vision, w_value, preferred_element_type=jnp.float32)  10.5 us
    reduce_sum x1, other arithmetic, prepare_rounds(): current_value = jnp.sum(all_gather(here_x, named_axis), 0)  9.07 us
    reduce_sum x1, other arithmetic, attend(): totals = jnp.sum(powers, axis=-1)  8.49 us
  transfers between devices with their start and end apart: 4, of which 2 were waited for; matrix products, arithmetic and copies ran while one was open for 4% of the time, Pallas kernels for 0%

profile of v1, /device:TPU:0, one launch (start us, length us, event | category | flops | bytes accessed | tf_op | source)
XLA Modules:
  0.0 266.3 jit_solution(15861211125281841099)
XLA Ops:
  6.5 0.0 copy-start
  6.5 10.6 %convolution_convert_fusion = bf16[512,512]{0,1:T(8,128)(2,1)} fusion(bf16[512,7680]{1,0:T(8,128)(2,1)} %param.5, bf16[7680,512]{1,0:T(8,128)(2,1)} %param.6), kind=kOutput, calls=%fused_computation.7 | convolution fusion | flops 4026793984 | bytes 16252928 | tf_op jit(solution)/shard_map/dot_general | solution.py:59
  17.1 4.5 %all-to-all-start.1 = ((bf16[512,4,128]{0,2,1:T(8,128)(2,1)}), bf16[512,4,128]{0,2,1:T(8,128)(2,1)S(1)}, u32[]{:S(2)}, u32[]{:S(2)}) async-start(bf16[512,4,128]{0,2,1:T(8,128)(2,1)} %bitcast.2), calls=%async_computation.1 | async-start | bytes 1048576 | tf_op jit(solution)/shard_map/all_to_all | solution.py:62
  21.7 10.5 %convolution_convert_fusion.1 = bf16[512,512]{0,1:T(8,128)(2,1)} fusion(bf16[512,7680]{1,0:T(8,128)(2,1)} %param.5, bf16[7680,512]{1,0:T(8,128)(2,1)} %param.7), kind=kOutput, calls=%fused_computation.8 | convolution fusion | flops 4026793984 | bytes 16252928 | tf_op jit(solution)/shard_map/dot_general | solution.py:60
  32.2 0.0 all-to-all-done.1
  32.2 4.8 %all-to-all-start = ((bf16[512,4,128]{0,2,1:T(8,128)(2,1)}), bf16[512,4,128]{0,2,1:T(8,128)(2,1)S(1)}, u32[]{:S(2)}, u32[]{:S(2)}) async-start(bf16[512,4,128]{0,2,1:T(8,128)(2,1)} %bitcast), calls=%async_computation | async-start | bytes 1048576 | tf_op jit(solution)/shard_map/all_to_all | solution.py:63
  37.0 0.0 copy-done.1
  37.0 26.5 %all_gather.7 = bf16[256,1024]{1,0:T(8,128)(2,1)S(1)} all-gather(bf16[8,1024]{1,0:T(8,128)(2,1)S(1)} %copy-done.1), channel_id=1, replica_groups=mesh['seq'=32,'head'=4] {'seq'}, dimensions={0}, use_global_device_ids=true | all-gather | bytes 540672 | tf_op jit(solution)/shard_map/all_gather | solution.py:65
  63.5 0.2 copy.18
  63.7 0.3 copy.17
  64.0 0.0 all-to-all-done
  64.0 0.4 copy.16
  64.4 0.4 reshape.78
  64.8 8.0 %bitcast_reduce_fusion = (f32[8,256]{1,0:T(8,128)S(1)}, f32[2048,256,8]{1,0,2:T(8,128)}) fusion(bf16[2048,128,1]{1,0,2:T(8,128)(2,1)S(1)} %bitcast.62, bf16[256,8,128]{0,2,1:T(8,128)(2,1)S(1)} %bitcast.61), kind=kOutput, calls=%fused_computation.1 | convolution fusion | flops 1082128384 | bytes 17833984 | tf_op jit(solution)/shard_map/tkgd,nkd->kgtn/dot_general | solution.py:40
  72.8 66.3 %pmax.7 = f32[256,8]{0,1:T(8,128)S(1)} all-reduce(f32[256,8]{0,1:T(8,128)S(1)} %bitcast.65), channel_id=1, replica_groups=mesh['seq'=32,'head'=4] {'seq'}, use_global_device_ids=true, to_apply=%region_1.0 | all-reduce | flops 2048 | bytes 16384 | tf_op jit(solution)/shard_map/pmax | solution.py:67
  139.1 8.5 %fusion.1 = f32[8,256]{1,0:T(8,128)S(1)} fusion(f32[2048,256,8]{1,0,2:T(8,128)} %get-tuple-element.8, f32[8,256]{1,0:T(8,128)S(1)} %get-tuple-element.7), kind=kLoop, calls=%fused_computation.3 | loop fusion | flops 12580864 | bytes 16793600 | tf_op jit(solution)/shard_map/reduce_sum | solution.py:45
  147.6 7.4 %fusion.4 = f32[128,8,256]{2,0,1:T(8,128)S(1)} fusion(bf16[2048,128,1]{0,1,2:T(8,128)(2,1)S(1)} %reshape.78, f32[2048,256,8]{1,0,2:T(8,128)} %get-tuple-element.8, f32[8,256]{1,0:T(8,128)S(1)} %get-tuple-element.7), kind=kOutput, calls=%fused_computation.6 | convolution fusion | flops 1086324736 | bytes 18358272 | tf_op jit(solution)/shard_map/kgtn,nkd->tkgd/dot_general | solution.py:46
  155.0 0.3 copy.22
  155.4 0.1 copy.21
  155.5 1.3 mul.37
  156.8 1.4 mul.38
  158.2 0.9 multiply_convert_fusion
  159.1 0.0 all-gather.2.cloned.1.call-update
  159.2 0.0 reduce-scatter.2.cloned.1.call-start
  159.2 64.8 %psum.7 = bf16[256,8]{0,1:T(8,128)(2,1)S(1)} all-reduce(bf16[256,8]{0,1:T(8,128)(2,1)S(1)} %get-tuple-element.5), channel_id=1, replica_groups=mesh['seq'=32,'head'=4] {'seq'}, use_global_device_ids=true, to_apply=%region_4.0 | all-reduce | flops 2048 | bytes 8192 | tf_op jit(solution)/shard_map/psum | solution.py:70
  224.0 5.1 %all-gather.2.cloned.1.call-done = bf16[32,256,1024]{2,1,0:T(8,128)(2,1)} async-done(((bf16[1,256,1024]{2,1,0:T(8,128)(2,1)}), bf16[32,256,1024]{2,1,0:T(8,128)(2,1)}) %all-gather.2.cloned.1.call-update) | async-done | bytes 16777232 | tf_op jit(solution)/shard_map/all_gather | solution.py:12
  229.1 9.1 %reduce_sum.23 = bf16[256,1024]{1,0:T(8,128)(2,1)S(1)} reduce(bf16[32,256,1024]{2,1,0:T(8,128)(2,1)} %all-gather.2.cloned.1.call-done, bf16[]{:T(256)} %constant.6.clone.1), dimensions={0}, to_apply=%region_2.0 | reduce | flops 8126464 | bytes 17301506 | tf_op jit(solution)/shard_map/reduce_sum | solution.py:12
  238.2 0.2 copy.26
  238.4 0.1 fusion.6
  238.5 1.0 convolution_convert_fusion.2
  239.5 0.0 reduce-scatter.2.cloned.1.call-update
  239.5 19.9 %reduce-scatter.2.cloned.1.call-done = bf16[64,256]{1,0:T(8,128)(2,1)} async-done(((bf16[256,256]{1,0:T(8,128)(2,1)}), bf16[64,256]{1,0:T(8,128)(2,1)}) %reduce-scatter.2.cloned.1.call-update) | async-done | bytes 32784 | tf_op jit(solution)/shard_map/reduce_scatter | solution.py:74
  (5 shorter events, 0.0 us)
Async XLA Ops:
  6.5 232.0 %copy-start = (bf16[1024,256]{1,0:T(8,128)(2,1)S(1)}, bf16[1024,256]{1,0:T(8,128)(2,1)}, u32[]{:S(2)}) copy-start(bf16[1024,256]{1,0:T(8,128)(2,1)} %param.9) | copy-start | bytes 1572868
  17.1 19.9 %copy-start.1 = (bf16[8,1024]{1,0:T(8,128)(2,1)S(1)}, bf16[8,1024]{1,0:T(8,128)(2,1)}, u32[]{:S(2)}) copy-start(bf16[8,1024]{1,0:T(8,128)(2,1)} %param.8) | copy-start | bytes 49156
  17.1 15.1 %all-to-all-start.1 = ((bf16[512,4,128]{0,2,1:T(8,128)(2,1)}), bf16[512,4,128]{0,2,1:T(8,128)(2,1)S(1)}, u32[]{:S(2)}, u32[]{:S(2)}) async-start(bf16[512,4,128]{0,2,1:T(8,128)(2,1)} %bitcast.2), calls=%async_computation.1 | async-start | bytes 1048576 | tf_op jit(solution)/shard_map/all_to_all | solution.py:62
  32.2 31.8 %all-to-all-start = ((bf16[512,4,128]{0,2,1:T(8,128)(2,1)}), bf16[512,4,128]{0,2,1:T(8,128)(2,1)S(1)}, u32[]{:S(2)}, u32[]{:S(2)}) async-start(bf16[512,4,128]{0,2,1:T(8,128)(2,1)} %bitcast), calls=%async_computation | async-start | bytes 1048576 | tf_op jit(solution)/shard_map/all_to_all | solution.py:63
  37.0 192.1 %all-gather.2.cloned.1.call-start = ((), (), s32[]{:S(2)}) async-start(), calls=%async_computation.3 | async-start | bytes 17301504 | tf_op jit(solution)/shard_map/all_gather | solution.py:12
  159.2 100.3 %reduce-scatter.2.cloned.1.call-start = ((), (), s32[]{:S(2)}) async-start(), calls=%async_computation.4 | async-start | bytes 163840 | tf_op jit(solution)/shard_map/reduce_scatter | solution.py:74
Sparse Core Ops, SparseCore 0:
  159.3 69.7 all-gather.1
  239.6 19.7 reduce-scatter.1
